TPU v7x, 256 devices: a whole 4x4x8 slice. The times are simulated.
256 devices in a mesh: section: 8 (over y, core), rows: 32 (over x, z).
Axes of the slice: x: 4, y: 4, z: 8, core: 2. Of those that a mesh axis runs over, the one named last changes fastest.
Arguments:
- grad_in: bfloat16 [8, 8192, 256], P('section', 'rows'), may hold values from -6 to 6
- grad_last: bfloat16 [8192, 256], P('rows'), may hold values from -6 to 6
- support: bfloat16 [8, 2, 2, 8192, 256], P('section', None, None, 'rows'), may hold values from -6 to 6
- preact: bfloat16 [8, 2, 2, 8192, 256], P('section', None, None, 'rows'), may hold values from -6 to 6
- weights: bfloat16 [8, 2, 256, 256], P('section'), may hold values from -0.375 to 0.375
- tile_vals: bfloat16 [8, 2, 3072, 128, 128], P('section', None, 'rows'), may hold values from -0.078125 to 0.078125
- tile_row: int32 [8, 2, 3072], P('section', None, 'rows'), may hold values from 0 to 1
- tile_col: int32 [8, 2, 3072], P('section', None, 'rows'), may hold values from 0 to 63, as said below
- tile_count: int32 [8, 2, 32], P('section', None, 'rows'), may hold values from 48 to 96, as said below
Outputs:
- handoff: bfloat16 [2, 8, 8192, 256], P(None, 'section', 'rows')
- init_grad: float32 [8, 2, 8192, 256], P('section', None, 'rows')
- weight_grad: float32 [8, 2, 256, 256], P('section')
Inputs may be any that keep to these rules, and one draw needn't show every extreme that they name: tile_count[s, t, d] is the number of live entries in device d's list; in every section and micro-batch some device has all 96 live. `tile_col`: for every section, micro-batch and pair of devices d and o with o != d, all entries of device d's list (live or padding) whose column tile lies in device o's rows name one and the same of o's 2 row tiles.
All inputs are finite; a program needn't handle non-finite values.
Results may differ from a plain program's by a relative error of at most 0.0066.
Values may be sent and summed in bfloat16 or wider, within the bound.
A program may use at most 128 MiB of HBM per device.

v0:
```python
import jax
import jax.numpy as jnp
from jax import lax
from jax.sharding import PartitionSpec as P

ALPHA = 0.1
BETA_SCALE = 0.5


def passed_along(block, axis, distance):
    devices = range(lax.axis_size(axis))
    route = [(i - distance, i) for i in devices if i - distance in devices]
    return lax.ppermute(block, axis, route)


def tile_product(gathered, values, row_local, index, count, row_tiles):
    tile = values.shape[-1]
    width = gathered.shape[-1]
    blocks = gathered.reshape(-1, tile, width)[index]
    products = jnp.einsum("kab,kbf->kaf", values, blocks, preferred_element_type=jnp.float32)
    live = jnp.arange(index.shape[0]) < count
    select = ((row_local[None, :] == jnp.arange(row_tiles)[:, None]) & live[None, :]).astype(
        jnp.float32
    )
    summed = jnp.einsum("ik,kaf->iaf", select, products, precision=lax.Precision.HIGHEST)
    return summed.reshape(row_tiles * tile, width)


def shards(grad_in, grad_last, support, preact, weights, tile_vals, tile_row, tile_col, tile_count):
    section = lax.axis_index("section")
    sections = lax.axis_size("section")
    ticks = support.shape[1]
    layers = support.shape[2]
    rows_dev, width = grad_last.shape
    tile = tile_vals.shape[-1]
    row_tiles = rows_dev // tile
    weight_acc = [jnp.zeros((width, width), jnp.float32) for layer in range(layers)]
    handed = []
    initial = []
    for tick in range(ticks):
        if tick == 0:
            grad = grad_in[0]
        else:
            passed = passed_along(handed[-1], "section", -1)
            grad = jnp.where(section == sections - 1, grad_last, passed)
        columns = tile_col[0, tick]
        count = tile_count[0, tick, 0]
        toward = jnp.zeros((rows_dev, width), jnp.float32)
        for layer in reversed(range(layers)):
            beta = jnp.log(BETA_SCALE / (layers * section + layer + 1).astype(jnp.float32) + 1.0)
            weight = weights[0, layer]
            masked = jnp.where(preact[0, tick, layer] > 0, grad, jnp.zeros_like(grad))
            term = beta * jnp.dot(
                support[0, tick, layer].T, masked, preferred_element_type=jnp.float32
            )
            weight_acc[layer] = weight_acc[layer] + lax.psum(term, "rows")
            image = (
                (1.0 - beta) * masked.astype(jnp.float32)
                + beta * jnp.dot(masked, weight.T, preferred_element_type=jnp.float32)
            ).astype(jnp.bfloat16)
            toward = toward + ALPHA * image.astype(jnp.float32)
            gathered = lax.all_gather(image, "rows", axis=0, tiled=True)
            spread = tile_product(
                gathered, tile_vals[0, tick], tile_row[0, tick], columns, count, row_tiles
            )
            grad = ((1.0 - ALPHA) * spread).astype(jnp.bfloat16)
        handed.append(grad)
        initial.append(toward)
    return (jnp.stack(handed)[:, None], jnp.stack(initial)[None], jnp.stack(weight_acc)[None])


def solution(mesh):
    return jax.shard_map(
        shards,
        mesh=mesh,
        in_specs=(
            P("section", "rows", None),
            P("rows", None),
            P("section", None, None, "rows", None),
            P("section", None, None, "rows", None),
            P("section", None, None, None),
            P("section", None, "rows", None, None),
            P("section", None, "rows"),
            P("section", None, "rows"),
            P("section", None, "rows"),
        ),
        out_specs=(
            P(None, "section", "rows", None),
            P("section", None, "rows", None),
            P("section", None, None, None),
        ),
        check_vma=False,
    )
```

profile of v0, /device:TPU:8, one launch (start us, length us, event | category | flops | bytes accessed | tf_op | source)
XLA Modules:
  0.0 648.4 jit_solution(17739819495514293798)
XLA Ops:
  7.3 2.1 fusion.15
  13.0 82.8 %all-gather.5.cloned.1.call-done = bf16[8192,256]{1,0:T(8,128)(2,1)} async-done(((bf16[256,256]{1,0:T(8,128)(2,1)}), bf16[8192,256]{1,0:T(8,128)(2,1)}) %all-gather.5.cloned.1.call-update) | async-done | bytes 4194320 | tf_op jit(solution)/shard_map/all_gather | solution.py:62
  95.8 8.1 %gather_fusion = bf16[96,128,256]{2,1,0:T(8,128)(2,1)} fusion(bf16[64,128,256]{2,1,0:T(8,128)(2,1)} %bitcast.141, s32[1024]{0:T(1024)S(1)} %pad_clamp_fusion.1), kind=kCustom, calls=%fused_computation | custom fusion | bytes 12583296 | tf_op jit(solution)/shard_map/gather | solution.py:19
  103.9 10.1 %convolution_bitcast_fusion.3 = f32[96,128,256]{1,2,0:T(8,128)} fusion(bf16[96,128,256]{2,1,0:T(8,128)(2,1)} %gather_fusion, bf16[1,2,96,128,128]{4,3,2,1,0:T(8,128)(2,1)} %param.14), kind=kOutput, calls=%fused_computation.7 | convolution fusion | flops 805306368 | bytes 22020096 | tf_op jit(solution)/shard_map/kab,kbf->kaf/dot_general | solution.py:20
  114.0 12.8 %copy.38 = f32[96,128,256]{2,0,1:T(8,128)} copy(f32[96,128,256]{1,2,0:T(8,128)} %convolution_bitcast_fusion.3) | data formatting | bytes 25165824 | tf_op jit(solution)/shard_map/kab,kbf->kaf/dot_general | solution.py:20
  126.7 7.1 %fusion.65 = f32[2,128,256]{2,0,1:T(2,128)S(1)} fusion(f32[96,128,256]{2,0,1:T(8,128)} %copy.38, pred[96]{0:T(512)(128)(4,1)S(1)} %iota_compare_fusion.1, s32[96]{0:T(128)S(1)} %get-tuple-element.18), kind=kOutput, calls=%fused_computation.97 | convolution fusion | flops 75497856 | bytes 12845536 | tf_op jit(solution)/shard_map/ik,kaf->iaf/dot_general | solution.py:25
  135.0 78.9 %all-gather.7.cloned.1.call-done = bf16[8192,256]{1,0:T(8,128)(2,1)} async-done(((bf16[256,256]{1,0:T(8,128)(2,1)}), bf16[8192,256]{1,0:T(8,128)(2,1)}) %all-gather.7.cloned.1.call-update) | async-done | bytes 4194320 | tf_op jit(solution)/shard_map/all_gather | solution.py:62
  213.9 8.1 %gather_fusion.1 = bf16[96,128,256]{2,1,0:T(8,128)(2,1)} fusion(bf16[64,128,256]{2,1,0:T(8,128)(2,1)} %bitcast.144, s32[1024]{0:T(1024)S(1)} %pad_clamp_fusion.1), kind=kCustom, calls=%fused_computation.1 | custom fusion | bytes 12583296 | tf_op jit(solution)/shard_map/gather | solution.py:19
  222.0 10.1 %convolution_bitcast_fusion.2 = f32[96,128,256]{1,2,0:T(8,128)} fusion(bf16[96,128,256]{2,1,0:T(8,128)(2,1)} %gather_fusion.1, bf16[1,2,96,128,128]{4,3,2,1,0:T(8,128)(2,1)} %param.14), kind=kOutput, calls=%fused_computation.6 | convolution fusion | flops 805306368 | bytes 22020096 | tf_op jit(solution)/shard_map/kab,kbf->kaf/dot_general | solution.py:20
  232.1 12.8 %copy.41 = f32[96,128,256]{2,0,1:T(8,128)} copy(f32[96,128,256]{1,2,0:T(8,128)} %convolution_bitcast_fusion.2) | data formatting | bytes 25165824 | tf_op jit(solution)/shard_map/kab,kbf->kaf/dot_general | solution.py:20
  244.9 7.1 %fusion.63 = f32[2,128,256]{2,0,1:T(2,128)S(1)} fusion(f32[96,128,256]{2,0,1:T(8,128)} %copy.41, pred[96]{0:T(512)(128)(4,1)S(1)} %iota_compare_fusion.1, s32[96]{0:T(128)S(1)} %get-tuple-element.18), kind=kOutput, calls=%fused_computation.95 | convolution fusion | flops 75497856 | bytes 12845536 | tf_op jit(solution)/shard_map/ik,kaf->iaf/dot_general | solution.py:25
  252.0 1.9 collective-permute-start
  253.9 2.5 collective-permute-done
  259.7 78.0 %all-gather.9.cloned.1.call-done = bf16[8192,256]{1,0:T(8,128)(2,1)} async-done(((bf16[256,256]{1,0:T(8,128)(2,1)}), bf16[8192,256]{1,0:T(8,128)(2,1)}) %all-gather.9.cloned.1.call-update) | async-done | bytes 4194320 | tf_op jit(solution)/shard_map/all_gather | solution.py:62
  337.7 8.1 %gather_fusion.2 = bf16[96,128,256]{2,1,0:T(8,128)(2,1)} fusion(bf16[64,128,256]{2,1,0:T(8,128)(2,1)} %bitcast.143, s32[1024]{0:T(1024)S(1)} %pad_clamp_fusion), kind=kCustom, calls=%fused_computation.2 | custom fusion | bytes 12583296 | tf_op jit(solution)/shard_map/gather | solution.py:19
  345.8 10.1 %convolution_bitcast_fusion.1 = f32[96,128,256]{1,2,0:T(8,128)} fusion(bf16[96,128,256]{2,1,0:T(8,128)(2,1)} %gather_fusion.2, bf16[1,2,96,128,128]{4,3,2,1,0:T(8,128)(2,1)} %param.14), kind=kOutput, calls=%fused_computation.5 | convolution fusion | flops 805306368 | bytes 22020096 | tf_op jit(solution)/shard_map/kab,kbf->kaf/dot_general | solution.py:20
  355.9 12.8 %copy.44 = f32[96,128,256]{2,0,1:T(8,128)} copy(f32[96,128,256]{1,2,0:T(8,128)} %convolution_bitcast_fusion.1) | data formatting | bytes 25165824 | tf_op jit(solution)/shard_map/kab,kbf->kaf/dot_general | solution.py:20
  368.6 7.0 %fusion.61 = f32[2,128,256]{2,0,1:T(2,128)S(1)} fusion(f32[96,128,256]{2,0,1:T(8,128)} %copy.44, pred[96]{0:T(512)(128)(4,1)S(1)} %iota_compare_fusion, s32[96]{0:T(128)S(1)} %get-tuple-element.17), kind=kOutput, calls=%fused_computation.93 | convolution fusion | flops 75497856 | bytes 12845536 | tf_op jit(solution)/shard_map/ik,kaf->iaf/dot_general | solution.py:25
  379.8 141.9 %all-reduce.3.cloned.1.call-done = (f32[256,256]{0,1:T(8,128)}, f32[256,256]{0,1:T(8,128)}) async-done(((f32[256,256]{0,1:T(8,128)}, f32[256,256]{0,1:T(8,128)}), (f32[256,256]{0,1:T(8,128)}, f32[256,256]{0,1:T(8,128)})) %all-reduce.3.cloned.1.call-update) | async-done | bytes 524304 | tf_op jit(solution)/shard_map/psum | solution.py:56
  523.7 79.4 %all-gather.11.cloned.1.call-done = bf16[8192,256]{1,0:T(8,128)(2,1)} async-done(((bf16[256,256]{1,0:T(8,128)(2,1)}), bf16[8192,256]{1,0:T(8,128)(2,1)}) %all-gather.11.cloned.1.call-update) | async-done | bytes 4194320 | tf_op jit(solution)/shard_map/all_gather | solution.py:62
  603.1 8.1 %gather_fusion.3 = bf16[96,128,256]{2,1,0:T(8,128)(2,1)} fusion(bf16[64,128,256]{2,1,0:T(8,128)(2,1)} %bitcast.142, s32[1024]{0:T(1024)S(1)} %pad_clamp_fusion), kind=kCustom, calls=%fused_computation.3 | custom fusion | bytes 12583296 | tf_op jit(solution)/shard_map/gather | solution.py:19
  611.2 10.1 %convolution_bitcast_fusion = f32[96,128,256]{1,2,0:T(8,128)} fusion(bf16[96,128,256]{2,1,0:T(8,128)(2,1)} %gather_fusion.3, bf16[1,2,96,128,128]{4,3,2,1,0:T(8,128)(2,1)} %param.14), kind=kOutput, calls=%fused_computation.4 | convolution fusion | flops 805306368 | bytes 22020096 | tf_op jit(solution)/shard_map/kab,kbf->kaf/dot_general | solution.py:20
  621.3 12.8 %copy.47 = f32[96,128,256]{2,0,1:T(8,128)} copy(f32[96,128,256]{1,2,0:T(8,128)} %convolution_bitcast_fusion) | data formatting | bytes 25165824 | tf_op jit(solution)/shard_map/kab,kbf->kaf/dot_general | solution.py:20
  634.1 7.0 %fusion.59 = f32[2,128,256]{2,0,1:T(2,128)S(1)} fusion(f32[96,128,256]{2,0,1:T(8,128)} %copy.47, pred[96]{0:T(512)(128)(4,1)S(1)} %iota_compare_fusion, s32[96]{0:T(128)S(1)} %get-tuple-element.17), kind=kOutput, calls=%fused_computation.91 | convolution fusion | flops 75497856 | bytes 12845536 | tf_op jit(solution)/shard_map/ik,kaf->iaf/dot_general | solution.py:25
  (51 shorter events, 14.8 us)
Async XLA Ops:
  7.2 88.6 %all-gather.5.cloned.1.call-start = ((), (), s32[]{:S(2)}) async-start(), calls=%async_computation | async-start | bytes 4325376 | tf_op jit(solution)/shard_map/all_gather | solution.py:62
  9.4 204.6 %all-gather.7.cloned.1.call-start = ((), (), s32[]{:S(2)}) async-start(), calls=%async_computation.1 | async-start | bytes 4325376 | tf_op jit(solution)/shard_map/all_gather | solution.py:62
  126.7 7.1 %copy-start = (bf16[1,2,2,256,256]{4,3,2,1,0:T(8,128)(2,1)S(1)}, bf16[1,2,2,256,256]{4,3,2,1,0:T(8,128)(2,1)}, u32[]{:S(2)}) copy-start(bf16[1,2,2,256,256]{4,3,2,1,0:T(8,128)(2,1)} %param.12) | copy-start | bytes 1572868
  126.7 7.1 %copy-start.7 = (bf16[1,2,256,256]{3,2,1,0:T(8,128)(2,1)S(1)}, bf16[1,2,256,256]{3,2,1,0:T(8,128)(2,1)}, u32[]{:S(2)}) copy-start(bf16[1,2,256,256]{3,2,1,0:T(8,128)(2,1)} %param.13) | copy-start | bytes 786436
  134.8 202.9 %all-gather.9.cloned.1.call-start = ((), (), s32[]{:S(2)}) async-start(), calls=%async_computation.2 | async-start | bytes 4325376 | tf_op jit(solution)/shard_map/all_gather | solution.py:62
  244.9 11.6 %copy-start.5 = (bf16[256,256]{1,0:T(8,128)(2,1)S(1)}, bf16[256,256]{1,0:T(8,128)(2,1)}, u32[]{:S(2)}) copy-start(bf16[256,256]{1,0:T(8,128)(2,1)} %param.10) | copy-start | bytes 393220
  244.9 13.4 %copy-start.1 = (bf16[1,2,2,256,256]{4,3,2,1,0:T(8,128)(2,1)S(1)}, bf16[1,2,2,256,256]{4,3,2,1,0:T(8,128)(2,1)}, u32[]{:S(2)}) copy-start(bf16[1,2,2,256,256]{4,3,2,1,0:T(8,128)(2,1)} %param.11) | copy-start | bytes 1572868
  244.9 13.4 %copy-start.6 = (bf16[1,256,256]{2,1,0:T(8,128)(2,1)S(1)}, bf16[1,256,256]{2,1,0:T(8,128)(2,1)}, u32[]{:S(2)}) copy-start(bf16[1,256,256]{2,1,0:T(8,128)(2,1)} %param.9) | copy-start | bytes 393220
  252.0 4.4 collective-permute-start
  257.3 264.3 %all-reduce.3.cloned.1.call-start = ((), (), s32[]{:S(2)}) async-start(), calls=%async_computation.4 | async-start | bytes 1048576 | tf_op jit(solution)/shard_map/psum | solution.py:56
  368.6 9.3 %copy-start.2 = (bf16[256,256]{1,0:T(8,128)(2,1)S(1)}, bf16[256,256]{1,0:T(8,128)(2,1)}, u32[]{:S(2)}) copy-start(bf16[256,256]{1,0:T(8,128)(2,1)} %fusion.15) | copy-start | bytes 393220
  368.6 9.3 %copy-start.3 = (bf16[256,256]{1,0:T(8,128)(2,1)S(1)}, bf16[256,256]{1,0:T(8,128)(2,1)}, u32[]{:S(2)}) copy-start(bf16[256,256]{1,0:T(8,128)(2,1)} %fusion.16) | copy-start | bytes 393220
  368.6 9.3 %copy-start.4 = (bf16[256,256]{1,0:T(8,128)(2,1)S(1)}, bf16[256,256]{1,0:T(8,128)(2,1)}, u32[]{:S(2)}) copy-start(bf16[256,256]{1,0:T(8,128)(2,1)} %add_convert_fusion) | copy-start | bytes 393220
  376.7 226.5 %all-gather.11.cloned.1.call-start = ((), (), s32[]{:S(2)}) async-start(), calls=%async_computation.3 | async-start | bytes 4325376 | tf_op jit(solution)/shard_map/all_gather | solution.py:62
Sparse Core Ops, SparseCore 0:
  11.2 84.5 all-gather.4
  134.9 78.9 all-gather.6
  257.5 80.1 all-gather.8
  376.8 144.8 all-reduce.2
  524.5 78.6 all-gather.10
where the time goes:
time: 649 us; the launch traced here: 648 us
  waiting for transfers between devices  464 us (71%)
  local copies, waits for them, and re-layouts  86.5 us (13%)
  matrix products  75.5 us (12%)
  between operations  14.2 us (2%)
    all_gather x4, waiting for transfers between devices, shards(): gathered = lax.all_gather(image, 'rows', axis=0, tiled=True)  319 us
    psum x1, waiting for transfers between devices, shards(): weight_acc[layer] = weight_acc[layer] + lax.psum(term, 'rows')  142 us
    dot_general x4, local copies, waits for them, and re-layouts, tile_product(): jnp.einsum('kab,kbf->kaf', values, blocks, preferred_element_type=jnp.flo...  51 us
    dot_general x4, matrix products, tile_product(): jnp.einsum('kab,kbf->kaf', values, blocks, preferred_element_type=jnp.flo...  40.3 us
    gather x4, local copies, waits for them, and re-layouts, tile_product(): blocks = gathered.reshape(-1, tile, width)[index]  32.4 us
    dot_general x4, matrix products, tile_product(): jnp.einsum('ik,kaf->iaf', select, products, precision=lax.Precision.HIGHEST)  28.2 us
  transfers between devices with their start and end apart: 6, of which 6 were waited for; matrix products, arithmetic and copies ran while one was open for 2% of the time, Pallas kernels for 0%

commit v1 on v0

--- a/solution.py
+++ b/solution.py
@@ -53,7 +53,7 @@
             term = beta * jnp.dot(
                 support[0, tick, layer].T, masked, preferred_element_type=jnp.float32
             )
-            weight_acc[layer] = weight_acc[layer] + lax.psum(term, "rows")
+            weight_acc[layer] = weight_acc[layer] + jnp.sum(lax.all_gather(term, "rows"), axis=0)
             image = (
                 (1.0 - beta) * masked.astype(jnp.float32)
                 + beta * jnp.dot(masked, weight.T, preferred_element_type=jnp.float32)

time: 649 us -> 864 us (1.33)
  waiting for transfers between devices: 464 us -> 626 us
  local copies, waits for them, and re-layouts: 86.5 us -> 121 us
  other arithmetic: 5.81 us -> 18 us
    all_gather x0 -> x4, waiting for transfers between devices: none -> 314 us  [shards(): lax.all_gather(term, 'rows')]
    psum x1 -> x0, waiting for transfers between devices: 142 us -> none  [shards(): weight_acc[layer] = weight_acc[layer] + lax.psum(term, 'rows')]
    unnamed x17 -> x25, local copies, waits for them, and re-layouts: 1.03 us -> 35.1 us
    reduce_sum x0 -> x2, other arithmetic: none -> 14.1 us  [shards(): jnp.sum(lax.all_gather(term, 'rows'), axis=0)]
    all_gather x4, waiting for transfers between devices: 319 us -> 310 us  [shards(): gathered = lax.all_gather(image, 'rows', axis=0, tiled=True)]
  transfers between devices with their start and end apart: 6 -> 9, of which waited for: 6 -> 9; matrix products, arithmetic and copies ran while one was open for 2% -> 14% of each run, Pallas kernels for 0% -> 0%
where the time goes in v1:
time: 864 us; the launch traced here: 857 us
  waiting for transfers between devices  626 us (72%)
  local copies, waits for them, and re-layouts  121 us (14%)
  matrix products  74.1 us (9%)
  other arithmetic  18 us (2%)
  between operations  14.7 us (2%)
    all_gather x4, waiting for transfers between devices, shards(): lax.all_gather(term, 'rows')  314 us
    all_gather x4, waiting for transfers between devices, shards(): gathered = lax.all_gather(image, 'rows', axis=0, tiled=True)  310 us
    dot_general x4, local copies, waits for them, and re-layouts, tile_product(): jnp.einsum('kab,kbf->kaf', values, blocks, preferred_element_type=jnp.flo...  51.3 us
    dot_general x4, matrix products, tile_product(): jnp.einsum('kab,kbf->kaf', values, blocks, preferred_element_type=jnp.flo...  40.3 us
    unnamed x25, local copies, waits for them, and re-layouts  35.1 us
    gather x4, local copies, waits for them, and re-layouts, tile_product(): blocks = gathered.reshape(-1, tile, width)[index]  32.9 us
    dot_general x4, matrix products, tile_product(): jnp.einsum('ik,kaf->iaf', select, products, precision=lax.Precision.HIGHEST)  25.4 us
  transfers between devices with their start and end apart: 9, of which 9 were waited for; matrix products, arithmetic and copies ran while one was open for 14% of the time, Pallas kernels for 0%

profile of v1, /device:TPU:8, one launch (start us, length us, event | category | flops | bytes accessed | tf_op | source)
XLA Modules:
  0.0 857.4 jit_solution(2083172210814501196)
XLA Ops:
  13.0 82.2 %all-gather.13.cloned.1.call-done = bf16[8192,256]{1,0:T(8,128)(2,1)} async-done(((bf16[256,256]{1,0:T(8,128)(2,1)}), bf16[8192,256]{1,0:T(8,128)(2,1)}) %all-gather.13.cloned.1.call-update) | async-done | bytes 4194320 | tf_op jit(solution)/shard_map/all_gather | solution.py:62
  95.2 8.1 gather_fusion
  103.4 10.1 %convolution_bitcast_fusion.3 = f32[96,128,256]{1,2,0:T(8,128)} fusion(bf16[96,128,256]{2,1,0:T(8,128)(2,1)} %gather_fusion, bf16[1,2,96,128,128]{4,3,2,1,0:T(8,128)(2,1)} %param.14), kind=kOutput, calls=%fused_computation.11 | convolution fusion | flops 805306368 | bytes 22020096 | tf_op jit(solution)/shard_map/kab,kbf->kaf/dot_general | solution.py:20
  113.4 12.8 %copy.56 = f32[96,128,256]{2,0,1:T(8,128)} copy(f32[96,128,256]{1,2,0:T(8,128)} %convolution_bitcast_fusion.3) | data formatting | bytes 25165824 | tf_op jit(solution)/shard_map/kab,kbf->kaf/dot_general | solution.py:20
  134.5 78.9 %all-gather.15.cloned.1.call-done = bf16[8192,256]{1,0:T(8,128)(2,1)} async-done(((bf16[256,256]{1,0:T(8,128)(2,1)}), bf16[8192,256]{1,0:T(8,128)(2,1)}) %all-gather.15.cloned.1.call-update) | async-done | bytes 4194320 | tf_op jit(solution)/shard_map/all_gather | solution.py:62
  213.4 8.1 gather_fusion.1
  221.6 10.1 %convolution_bitcast_fusion.2 = f32[96,128,256]{1,2,0:T(8,128)} fusion(bf16[96,128,256]{2,1,0:T(8,128)(2,1)} %gather_fusion.1, bf16[1,2,96,128,128]{4,3,2,1,0:T(8,128)(2,1)} %param.14), kind=kOutput, calls=%fused_computation.10 | convolution fusion | flops 805306368 | bytes 22020096 | tf_op jit(solution)/shard_map/kab,kbf->kaf/dot_general | solution.py:20
  231.6 12.8 %copy.59 = f32[96,128,256]{2,0,1:T(8,128)} copy(f32[96,128,256]{1,2,0:T(8,128)} %convolution_bitcast_fusion.2) | data formatting | bytes 25165824 | tf_op jit(solution)/shard_map/kab,kbf->kaf/dot_general | solution.py:20
  259.9 77.4 %all-gather.17.cloned.1.call-done = bf16[8192,256]{1,0:T(8,128)(2,1)} async-done(((bf16[256,256]{1,0:T(8,128)(2,1)}), bf16[8192,256]{1,0:T(8,128)(2,1)}) %all-gather.17.cloned.1.call-update) | async-done | bytes 4194320 | tf_op jit(solution)/shard_map/all_gather | solution.py:62
  337.3 8.1 gather_fusion.2
  345.4 10.1 %convolution_bitcast_fusion.1 = f32[96,128,256]{1,2,0:T(8,128)} fusion(bf16[96,128,256]{2,1,0:T(8,128)(2,1)} %gather_fusion.2, bf16[1,2,96,128,128]{4,3,2,1,0:T(8,128)(2,1)} %param.14), kind=kOutput, calls=%fused_computation.9 | convolution fusion | flops 805306368 | bytes 22020096 | tf_op jit(solution)/shard_map/kab,kbf->kaf/dot_general | solution.py:20
  355.5 12.9 %copy.62 = f32[96,128,256]{2,0,1:T(8,128)} copy(f32[96,128,256]{1,2,0:T(8,128)} %convolution_bitcast_fusion.1) | data formatting | bytes 25165824 | tf_op jit(solution)/shard_map/kab,kbf->kaf/dot_general | solution.py:20
  368.3 7.1 fusion.59
  378.7 62.4 %all-gather.25.cloned.1.call-done = f32[8192,256]{0,1:T(8,128)} async-done(((f32[256,256]{0,1:T(8,128)}), f32[8192,256]{0,1:T(8,128)}) %all-gather.25.cloned.1.call-update) | async-done | bytes 8388624 | tf_op jit(solution)/shard_map/all_gather | solution.py:56
  441.1 10.1 %copy.75 = f32[32,8,32,256]{3,2,1,0:T(8,128)} copy(f32[32,8,32,256]{3,1,2,0:T(8,128)} %bitcast.171) | data formatting | bytes 16777216
  451.2 94.4 %all-gather.21.cloned.1.call-done = f32[8192,256]{0,1:T(8,128)} async-done(((f32[256,256]{0,1:T(8,128)}), f32[8192,256]{0,1:T(8,128)}) %all-gather.21.cloned.1.call-update) | async-done | bytes 8388624 | tf_op jit(solution)/shard_map/all_gather | solution.py:56
  545.5 10.1 %copy.73 = f32[32,8,32,256]{3,2,1,0:T(8,128)} copy(f32[32,8,32,256]{3,1,2,0:T(8,128)} %bitcast.172) | data formatting | bytes 16777216
  556.5 71.1 %all-gather.19.cloned.1.call-done = bf16[8192,256]{1,0:T(8,128)(2,1)} async-done(((bf16[256,256]{1,0:T(8,128)(2,1)}), bf16[8192,256]{1,0:T(8,128)(2,1)}) %all-gather.19.cloned.1.call-update) | async-done | bytes 4194320 | tf_op jit(solution)/shard_map/all_gather | solution.py:62
  627.6 8.6 %gather_fusion.3 = bf16[96,128,256]{2,1,0:T(8,128)(2,1)} fusion(bf16[64,128,256]{2,1,0:T(8,128)(2,1)} %bitcast.167, s32[1024]{0:T(1024)S(1)} %pad_clamp_fusion), kind=kCustom, calls=%fused_computation.3 | custom fusion | bytes 12583296 | tf_op jit(solution)/shard_map/gather | solution.py:19
  636.2 10.1 %convolution_bitcast_fusion = f32[96,128,256]{1,2,0:T(8,128)} fusion(bf16[96,128,256]{2,1,0:T(8,128)(2,1)} %gather_fusion.3, bf16[1,2,96,128,128]{4,3,2,1,0:T(8,128)(2,1)} %param.14), kind=kOutput, calls=%fused_computation.8 | convolution fusion | flops 805306368 | bytes 22020096 | tf_op jit(solution)/shard_map/kab,kbf->kaf/dot_general | solution.py:20
  646.3 12.9 %copy.65 = f32[96,128,256]{2,0,1:T(8,128)} copy(f32[96,128,256]{1,2,0:T(8,128)} %convolution_bitcast_fusion) | data formatting | bytes 25165824 | tf_op jit(solution)/shard_map/kab,kbf->kaf/dot_general | solution.py:20
  659.1 72.4 %all-gather.27.cloned.1.call-done = f32[8192,256]{0,1:T(8,128)} async-done(((f32[256,256]{0,1:T(8,128)}), f32[8192,256]{0,1:T(8,128)}) %all-gather.27.cloned.1.call-update) | async-done | bytes 8388624 | tf_op jit(solution)/shard_map/all_gather | solution.py:56
  743.6 7.2 bitcast_reduce_fusion
  750.8 84.7 %all-gather.23.cloned.1.call-done = f32[8192,256]{0,1:T(8,128)} async-done(((f32[256,256]{0,1:T(8,128)}), f32[8192,256]{0,1:T(8,128)}) %all-gather.23.cloned.1.call-update) | async-done | bytes 8388624 | tf_op jit(solution)/shard_map/all_gather | solution.py:56
  (72 shorter events, 60.2 us)
Async XLA Ops:
  7.2 88.1 %all-gather.13.cloned.1.call-start = ((), (), s32[]{:S(2)}) async-start(), calls=%async_computation | async-start | bytes 4325376 | tf_op jit(solution)/shard_map/all_gather | solution.py:62
  9.4 204.0 %all-gather.15.cloned.1.call-start = ((), (), s32[]{:S(2)}) async-start(), calls=%async_computation.1 | async-start | bytes 4325376 | tf_op jit(solution)/shard_map/all_gather | solution.py:62
  126.2 7.1 copy-start.6
  126.2 7.1 copy-start.8
  134.3 203.0 %all-gather.17.cloned.1.call-start = ((), (), s32[]{:S(2)}) async-start(), calls=%async_computation.2 | async-start | bytes 4325376 | tf_op jit(solution)/shard_map/all_gather | solution.py:62
  244.4 11.6 %copy-start.5 = (bf16[256,256]{1,0:T(8,128)(2,1)S(1)}, bf16[256,256]{1,0:T(8,128)(2,1)}, u32[]{:S(2)}) copy-start(bf16[256,256]{1,0:T(8,128)(2,1)} %param.10) | copy-start | bytes 393220
  244.4 12.6 %copy-start.7 = (bf16[1,2,2,256,256]{4,3,2,1,0:T(8,128)(2,1)S(1)}, bf16[1,2,2,256,256]{4,3,2,1,0:T(8,128)(2,1)}, u32[]{:S(2)}) copy-start(bf16[1,2,2,256,256]{4,3,2,1,0:T(8,128)(2,1)} %param.11) | copy-start | bytes 1572868
  244.4 12.6 %copy-start.9 = (bf16[1,256,256]{2,1,0:T(8,128)(2,1)S(1)}, bf16[1,256,256]{2,1,0:T(8,128)(2,1)}, u32[]{:S(2)}) copy-start(bf16[1,256,256]{2,1,0:T(8,128)(2,1)} %param.9) | copy-start | bytes 393220
  251.6 4.4 collective-permute-start
  256.9 184.2 %all-gather.25.cloned.1.call-start = ((), (), s32[]{:S(2)}) async-start(), calls=%async_computation.6 | async-start | bytes 8650752 | tf_op jit(solution)/shard_map/all_gather | solution.py:56
  258.0 287.6 %all-gather.21.cloned.1.call-start = ((), (), s32[]{:S(2)}) async-start(), calls=%async_computation.4 | async-start | bytes 8650752 | tf_op jit(solution)/shard_map/all_gather | solution.py:56
  259.0 368.6 %all-gather.19.cloned.1.call-start = ((), (), s32[]{:S(2)}) async-start(), calls=%async_computation.3 | async-start | bytes 4325376 | tf_op jit(solution)/shard_map/all_gather | solution.py:62
  368.3 10.3 %copy-start.1 = (bf16[256,256]{1,0:T(8,128)(2,1)S(1)}, bf16[256,256]{1,0:T(8,128)(2,1)}, u32[]{:S(2)}) copy-start(bf16[256,256]{1,0:T(8,128)(2,1)} %fusion.15) | copy-start | bytes 393220
  368.3 10.3 %copy-start.2 = (bf16[256,256]{1,0:T(8,128)(2,1)S(1)}, bf16[256,256]{1,0:T(8,128)(2,1)}, u32[]{:S(2)}) copy-start(bf16[256,256]{1,0:T(8,128)(2,1)} %fusion.16) | copy-start | bytes 393220
  376.4 355.2 %all-gather.27.cloned.1.call-start = ((), (), s32[]{:S(2)}) async-start(), calls=%async_computation.7 | async-start | bytes 8650752 | tf_op jit(solution)/shard_map/all_gather | solution.py:56
  377.4 458.2 %all-gather.23.cloned.1.call-start = ((), (), s32[]{:S(2)}) async-start(), calls=%async_computation.5 | async-start | bytes 8650752 | tf_op jit(solution)/shard_map/all_gather | solution.py:56
  545.5 10.1 %copy-start.3 = (bf16[256,256]{1,0:T(8,128)(2,1)S(1)}, bf16[256,256]{1,0:T(8,128)(2,1)}, u32[]{:S(2)}) copy-start(bf16[256,256]{1,0:T(8,128)(2,1)} %add_convert_fusion) | copy-start | bytes 393220
  545.5 10.1 %copy-start.4 = (bf16[256,256]{1,0:T(8,128)(2,1)S(1)}, bf16[256,256]{1,0:T(8,128)(2,1)}, u32[]{:S(2)}) copy-start(bf16[256,256]{1,0:T(8,128)(2,1)} %fusion.17) | copy-start | bytes 393220
  731.6 7.1 copy-start
Sparse Core Ops, SparseCore 0:
  10.6 84.5 all-gather.12
  134.4 78.9 all-gather.14
  257.1 80.1 all-gather.16
  340.2 100.8 all-gather.24
  444.0 101.4 all-gather.20
  548.0 79.5 all-gather.18
  630.6 100.8 all-gather.26
  734.0 101.4 all-gather.22
